TPU v7x, 32 devices: a whole 2x2x4 slice. The times are simulated.
32 devices in a mesh: wide: 8 (over y, x, core), narrow: 4 (over z).
Axes of the slice: x: 2, y: 2, z: 4, core: 2. Of those that a mesh axis runs over, the one named last changes fastest.
Arguments:
- tokens: bfloat16 [128, 512, 768], P(('wide', 'narrow')), may hold values from -6 to 6
- lengths: int32 [128], P(('wide', 'narrow')), may hold values from 128 to 512, as said below
- query_lengths: int32 [128], P(('wide', 'narrow')), may hold values from 2 to 64
- language_ids: int32 [128], P(('wide', 'narrow')), may hold values from 0 to 99
- position_table: bfloat16 [512, 768], P('wide', 'narrow'), may hold values from -3 to 3
- segment_table: bfloat16 [2, 768], replicated, may hold values from -3 to 3
- language_table: bfloat16 [100, 768], replicated, may hold values from -3 to 3
- query_weight: bfloat16 [768, 768], P('wide', 'narrow'), may hold values from -0.21875 to 0.21875
- key_weight: bfloat16 [768, 768], P('wide', 'narrow'), may hold values from -0.21875 to 0.21875
- value_weight: bfloat16 [768, 768], P('wide', 'narrow'), may hold values from -0.21875 to 0.21875
- output_weight: bfloat16 [768, 768], P('wide', 'narrow'), may hold values from -0.875 to 0.875
- query_bias: bfloat16 [768], replicated, may hold values from -2 to 2
- value_bias: bfloat16 [768], replicated, may hold values from -2 to 2
- output_bias: bfloat16 [768], replicated, may hold values from -2 to 2
- first_gain: bfloat16 [768], replicated, may hold values from 0.5 to 1.5
- first_shift: bfloat16 [768], replicated, may hold values from -2 to 2
- up_weight: bfloat16 [768, 3072], P('wide', 'narrow'), may hold values from -0.21875 to 0.21875
- up_bias: bfloat16 [3072], replicated, may hold values from -2 to 2
- down_weight: bfloat16 [3072, 768], P('wide', 'narrow'), may hold values from -0.109375 to 0.109375
- down_bias: bfloat16 [768], replicated, may hold values from -2 to 2
- second_gain: bfloat16 [768], replicated, may hold values from 0.5 to 1.5
- second_shift: bfloat16 [768], replicated, may hold values from -2 to 2
- cotangent: bfloat16 [128, 512, 768], P(('wide', 'narrow')), may hold values from -6 to 6
Outputs:
- layer_out: bfloat16 [128, 512, 768], P(('wide', 'narrow'))
- token_grad: bfloat16 [128, 512, 768], P(('wide', 'narrow'))
- position_grad: float32 [512, 768], P('wide', 'narrow')
- segment_grad: float32 [2, 768], replicated
- language_grad: float32 [100, 768], replicated
- query_weight_grad: float32 [768, 768], P('wide', 'narrow')
- key_weight_grad: float32 [768, 768], P('wide', 'narrow')
- value_weight_grad: float32 [768, 768], P('wide', 'narrow')
- output_weight_grad: float32 [768, 768], P('wide', 'narrow')
- query_bias_grad: float32 [768], replicated
- value_bias_grad: float32 [768], replicated
- output_bias_grad: float32 [768], replicated
- first_gain_grad: float32 [768], replicated
- first_shift_grad: float32 [768], replicated
- up_weight_grad: float32 [768, 3072], P('wide', 'narrow')
- up_bias_grad: float32 [3072], replicated
- down_weight_grad: float32 [3072, 768], P('wide', 'narrow')
- down_bias_grad: float32 [768], replicated
- second_gain_grad: float32 [768], replicated
- second_shift_grad: float32 [768], replicated
Inputs may be any that keep to these rules, and one draw needn't show every extreme that they name: Each pair has lengths live tokens, the rest are padding; some pair fills all 512 positions. `query_lengths`: A pair's queries lie within its live tokens.
All inputs are finite; a program needn't handle non-finite values.
Results may differ from a plain program's by a relative error of at most 0.015.
The roundings to bfloat16 on the way count: a program that leaves them out, or rounds other values in their place, can miss the bound.
Values may be sent and summed in bfloat16 or wider, within the bound.
No kernel may reach another device: no remote copies, remote signals or barrier semaphores. Data moves between devices by JAX's collectives and lax.ppermute only.
A program may use at most 256 MiB of HBM per device.

v0:
```python
import math

import jax
import jax.numpy as jnp
from jax import lax
from jax.sharding import PartitionSpec as P

H = 12
HD = 64


EPSILON = 1e-05


def normalize(inputs, scales, offset):
    average = jnp.mean(inputs, axis=-1, keepdims=True)
    centered = inputs - average
    spread = jnp.mean(centered * centered, axis=-1, keepdims=True)
    return centered * lax.rsqrt(spread + EPSILON) * scales + offset


def matmul(left_side, right_side):
    return jnp.dot(left_side, right_side, preferred_element_type=jnp.float32)


def matmul_first_t(left_side, right_side):
    return lax.dot_general(
        left_side, right_side, (((0,), (0,)), ((), ())), preferred_element_type=jnp.float32
    )


def matmul_second_t(left_side, right_side):
    return lax.dot_general(
        left_side, right_side, (((1,), (1,)), ((), ())), preferred_element_type=jnp.float32
    )


def exact_gelu(inputs):
    return jax.nn.gelu(inputs, approximate=False)


def split_heads(flattened, seq_count, seq_len):
    return (
        flattened.reshape(seq_count, seq_len, H, HD)
        .transpose(0, 2, 1, 3)
        .reshape(seq_count * H, seq_len, HD)
    )


def join_heads(blocks, seq_count, seq_len):
    return (
        blocks.reshape(seq_count, H, seq_len, HD)
        .transpose(0, 2, 1, 3)
        .reshape(seq_count * seq_len, H * HD)
    )


def assemble(stacked, wide_count, narrow_count):
    block_rows = stacked.shape[1]
    block_cols = stacked.shape[2]
    return (
        stacked.reshape(wide_count, narrow_count, block_rows, block_cols)
        .transpose(0, 2, 1, 3)
        .reshape(wide_count * block_rows, narrow_count * block_cols)
    )


def disassemble(whole, wide_count, narrow_count):
    block_rows = whole.shape[0] // wide_count
    block_cols = whole.shape[1] // narrow_count
    return (
        whole.reshape(wide_count, block_rows, narrow_count, block_cols)
        .transpose(0, 2, 1, 3)
        .reshape(wide_count * narrow_count, block_rows, block_cols)
    )


def block_scores(query_rows, key_rows, length):
    factor = 1.0 / math.sqrt(HD)
    products = matmul_second_t(query_rows, key_rows) * factor
    keeping = lax.broadcasted_iota(jnp.int32, products.shape, 1) < length
    return jnp.where(keeping, products, -1e30)


def attend_block(pieces):
    query_rows, key_rows, value_rows, length = pieces
    scores = block_scores(query_rows, key_rows, length)
    row_max = jnp.max(scores, axis=1, keepdims=True)
    weights = jnp.exp(scores - row_max)
    row_total = jnp.sum(weights, axis=1, keepdims=True)
    low_weights = (weights / row_total).astype(jnp.bfloat16)
    context = matmul(low_weights, value_rows)
    return (context, (row_max + jnp.log(row_total))[:, 0])


def attend_back(pieces):
    query_rows, key_rows, value_rows, length, log_totals, grad_context = pieces
    scores = block_scores(query_rows, key_rows, length)
    probabilities = jnp.exp(scores - log_totals[:, None])
    grad_probs = matmul_second_t(grad_context, value_rows)
    row_dots = jnp.sum(probabilities * grad_probs, axis=1, keepdims=True)
    grad_scores = (probabilities * (grad_probs - row_dots)).astype(jnp.bfloat16)
    factor = 1.0 / math.sqrt(HD)
    grad_query = matmul(grad_scores, key_rows) * factor
    grad_key = matmul_first_t(grad_scores, query_rows) * factor
    grad_value = matmul_first_t(probabilities.astype(jnp.bfloat16), grad_context)
    return (grad_query, grad_key, grad_value)


def on_device(
    tokens,
    lengths,
    query_lengths,
    language_ids,
    position_table,
    segment_table,
    language_table,
    query_weight,
    key_weight,
    value_weight,
    output_weight,
    query_bias,
    value_bias,
    output_bias,
    first_gain,
    first_shift,
    up_weight,
    up_bias,
    down_weight,
    down_bias,
    second_gain,
    second_shift,
    cotangent,
):
    seq_count, seq_len, features = tokens.shape
    row_count = seq_count * seq_len
    wide_count = lax.axis_size("wide")
    narrow_count = lax.axis_size("narrow")
    attention_stacks = (
        lax.all_gather(position_table[None], ("wide", "narrow"), axis=0, tiled=True),
        lax.all_gather(query_weight[None], ("wide", "narrow"), axis=0, tiled=True),
        lax.all_gather(key_weight[None], ("wide", "narrow"), axis=0, tiled=True),
        lax.all_gather(value_weight[None], ("wide", "narrow"), axis=0, tiled=True),
        lax.all_gather(output_weight[None], ("wide", "narrow"), axis=0, tiled=True),
    )
    position_full, query_full, key_full, value_full, output_full = [
        assemble(stacked, wide_count, narrow_count) for stacked in attention_stacks
    ]
    feedforward_stacks = (
        lax.all_gather(up_weight[None], ("wide", "narrow"), axis=0, tiled=True),
        lax.all_gather(down_weight[None], ("wide", "narrow"), axis=0, tiled=True),
    )
    up_full, down_full = [
        assemble(stacked, wide_count, narrow_count) for stacked in feedforward_stacks
    ]
    places = lax.broadcasted_iota(jnp.int32, (seq_count, seq_len), 1)
    passage = (places >= query_lengths[:, None])[:, :, None]
    segment_float = segment_table.astype(jnp.float32)
    segment_rows = jnp.where(passage, segment_float[1], segment_float[0])
    language_count = language_table.shape[0]
    language_hot = (
        language_ids[:, None] == lax.broadcasted_iota(jnp.int32, (seq_count, language_count), 1)
    ).astype(jnp.bfloat16)
    language_rows = matmul(language_hot, language_table)
    start = (
        tokens.astype(jnp.float32)
        + position_full.astype(jnp.float32)[None]
        + segment_rows
        + language_rows[:, None, :]
    )
    flattened = start.reshape(row_count, features)
    first_in = flattened.astype(jnp.bfloat16)
    query_rows = (matmul(first_in, query_full) + query_bias.astype(jnp.float32)).astype(
        jnp.bfloat16
    )
    key_rows = matmul(first_in, key_full).astype(jnp.bfloat16)
    value_rows = (matmul(first_in, value_full) + value_bias.astype(jnp.float32)).astype(
        jnp.bfloat16
    )
    query_heads = split_heads(query_rows, seq_count, seq_len)
    key_heads = split_heads(key_rows, seq_count, seq_len)
    value_heads = split_heads(value_rows, seq_count, seq_len)
    head_lengths = jnp.repeat(lengths, H)
    context_blocks, log_totals = lax.map(
        attend_block, (query_heads, key_heads, value_heads, head_lengths)
    )
    context = join_heads(context_blocks, seq_count, seq_len).astype(jnp.bfloat16)
    attended = matmul(context, output_full) + output_bias.astype(jnp.float32)
    first_out, first_pull = jax.vjp(
        normalize,
        flattened + attended,
        first_gain.astype(jnp.float32),
        first_shift.astype(jnp.float32),
    )
    second_in = first_out.astype(jnp.bfloat16)
    hidden_pre = matmul(second_in, up_full) + up_bias.astype(jnp.float32)
    hidden = exact_gelu(hidden_pre).astype(jnp.bfloat16)
    branch = matmul(hidden, down_full) + down_bias.astype(jnp.float32)
    final, second_pull = jax.vjp(
        normalize,
        first_out + branch,
        second_gain.astype(jnp.float32),
        second_shift.astype(jnp.float32),
    )
    layer_out = final.astype(jnp.bfloat16).reshape(seq_count, seq_len, features)
    feedforward_again = (
        lax.all_gather(up_weight[None], ("wide", "narrow"), axis=0, tiled=True),
        lax.all_gather(down_weight[None], ("wide", "narrow"), axis=0, tiled=True),
    )
    back_up, back_down = [
        assemble(stacked, wide_count, narrow_count) for stacked in feedforward_again
    ]
    attention_again = (
        lax.all_gather(query_weight[None], ("wide", "narrow"), axis=0, tiled=True),
        lax.all_gather(key_weight[None], ("wide", "narrow"), axis=0, tiled=True),
        lax.all_gather(value_weight[None], ("wide", "narrow"), axis=0, tiled=True),
        lax.all_gather(output_weight[None], ("wide", "narrow"), axis=0, tiled=True),
    )
    back_query, back_key, back_value, back_output = [
        assemble(stacked, wide_count, narrow_count) for stacked in attention_again
    ]
    grad_second, second_gain_grad, second_shift_grad = second_pull(
        cotangent.astype(jnp.float32).reshape(row_count, features)
    )
    grad_branch = grad_second.astype(jnp.bfloat16)
    down_bias_grad = jnp.sum(grad_branch.astype(jnp.float32), axis=0)
    down_weight_grad = matmul_first_t(hidden, grad_branch)
    gelu_value, gelu_pull = jax.vjp(exact_gelu, hidden_pre)
    grad_hidden = gelu_pull(matmul_second_t(grad_branch, back_down))[0].astype(jnp.bfloat16)
    up_bias_grad = jnp.sum(grad_hidden.astype(jnp.float32), axis=0)
    up_weight_grad = matmul_first_t(second_in, grad_hidden)
    grad_first_out = grad_second + matmul_second_t(grad_hidden, back_up)
    grad_first, first_gain_grad, first_shift_grad = first_pull(grad_first_out)
    grad_attended = grad_first.astype(jnp.bfloat16)
    output_bias_grad = jnp.sum(grad_attended.astype(jnp.float32), axis=0)
    output_weight_grad = matmul_first_t(context, grad_attended)
    grad_context = matmul_second_t(grad_attended, back_output).astype(jnp.bfloat16)
    grad_query_blocks, grad_key_blocks, grad_value_blocks = lax.map(
        attend_back,
        (
            query_heads,
            key_heads,
            value_heads,
            head_lengths,
            log_totals,
            split_heads(grad_context, seq_count, seq_len),
        ),
    )
    grad_query = join_heads(grad_query_blocks, seq_count, seq_len).astype(jnp.bfloat16)
    grad_key = join_heads(grad_key_blocks, seq_count, seq_len).astype(jnp.bfloat16)
    grad_value = join_heads(grad_value_blocks, seq_count, seq_len).astype(jnp.bfloat16)
    query_bias_grad = jnp.sum(grad_query.astype(jnp.float32), axis=0)
    value_bias_grad = jnp.sum(grad_value.astype(jnp.float32), axis=0)
    query_weight_grad = matmul_first_t(first_in, grad_query)
    key_weight_grad = matmul_first_t(first_in, grad_key)
    value_weight_grad = matmul_first_t(first_in, grad_value)
    grad_start = (
        grad_first
        + matmul_second_t(grad_query, back_query)
        + matmul_second_t(grad_key, back_key)
        + matmul_second_t(grad_value, back_value)
    )
    token_grad = grad_start.astype(jnp.bfloat16).reshape(seq_count, seq_len, features)
    grad_start_pairs = grad_start.reshape(seq_count, seq_len, features)
    position_local = jnp.sum(grad_start_pairs, axis=0)
    segment_local = jnp.stack(
        [
            jnp.sum(jnp.where(passage, 0.0, grad_start_pairs), axis=(0, 1)),
            jnp.sum(jnp.where(passage, grad_start_pairs, 0.0), axis=(0, 1)),
        ]
    )
    language_local = lax.dot_general(
        language_hot.astype(jnp.float32),
        jnp.sum(grad_start_pairs, axis=1),
        (((0,), (0,)), ((), ())),
        precision=lax.Precision.HIGHEST,
    )
    attention_blocks = (
        lax.psum_scatter(
            disassemble(position_local, wide_count, narrow_count),
            ("wide", "narrow"),
            scatter_dimension=0,
            tiled=True,
        ),
        lax.psum_scatter(
            disassemble(query_weight_grad, wide_count, narrow_count),
            ("wide", "narrow"),
            scatter_dimension=0,
            tiled=True,
        ),
        lax.psum_scatter(
            disassemble(key_weight_grad, wide_count, narrow_count),
            ("wide", "narrow"),
            scatter_dimension=0,
            tiled=True,
        ),
        lax.psum_scatter(
            disassemble(value_weight_grad, wide_count, narrow_count),
            ("wide", "narrow"),
            scatter_dimension=0,
            tiled=True,
        ),
        lax.psum_scatter(
            disassemble(output_weight_grad, wide_count, narrow_count),
            ("wide", "narrow"),
            scatter_dimension=0,
            tiled=True,
        ),
    )
    attention_sums = [summed_block[0] for summed_block in attention_blocks]
    feedforward_blocks = (
        lax.psum_scatter(
            disassemble(up_weight_grad, wide_count, narrow_count),
            ("wide", "narrow"),
            scatter_dimension=0,
            tiled=True,
        ),
        lax.psum_scatter(
            disassemble(down_weight_grad, wide_count, narrow_count),
            ("wide", "narrow"),
            scatter_dimension=0,
            tiled=True,
        ),
    )
    feedforward_sums = [summed_block[0] for summed_block in feedforward_blocks]
    small_sums = lax.psum(
        (
            segment_local,
            language_local,
            query_bias_grad,
            value_bias_grad,
            output_bias_grad,
            first_gain_grad,
            first_shift_grad,
            up_bias_grad,
            down_bias_grad,
            second_gain_grad,
            second_shift_grad,
        ),
        ("wide", "narrow"),
    )
    return (
        layer_out,
        token_grad,
        attention_sums[0],
        small_sums[0],
        small_sums[1],
        attention_sums[1],
        attention_sums[2],
        attention_sums[3],
        attention_sums[4],
        small_sums[2],
        small_sums[3],
        small_sums[4],
        small_sums[5],
        small_sums[6],
        feedforward_sums[0],
        small_sums[7],
        feedforward_sums[1],
        small_sums[8],
        small_sums[9],
        small_sums[10],
    )


def solution(mesh):
    return jax.shard_map(
        on_device,
        mesh=mesh,
        in_specs=(
            P(("wide", "narrow"), None, None),
            P(("wide", "narrow")),
            P(("wide", "narrow")),
            P(("wide", "narrow")),
            P("wide", "narrow"),
            P(),
            P(),
            P("wide", "narrow"),
            P("wide", "narrow"),
            P("wide", "narrow"),
            P("wide", "narrow"),
            P(),
            P(),
            P(),
            P(),
            P(),
            P("wide", "narrow"),
            P(),
            P("wide", "narrow"),
            P(),
            P(),
            P(),
            P(("wide", "narrow"), None, None),
        ),
        out_specs=(
            P(("wide", "narrow"), None, None),
            P(("wide", "narrow"), None, None),
            P("wide", "narrow"),
            P(),
            P(),
            P("wide", "narrow"),
            P("wide", "narrow"),
            P("wide", "narrow"),
            P("wide", "narrow"),
            P(),
            P(),
            P(),
            P(),
            P(),
            P("wide", "narrow"),
            P(),
            P("wide", "narrow"),
            P(),
            P(),
            P(),
        ),
        check_vma=False,
    )
```

profile of v0, /device:TPU:0, one launch (start us, length us, event | category | flops | bytes accessed | tf_op | source)
XLA Modules:
  0.0 2180.7 jit_solution(14981579719575982084)
XLA Ops:
  12.8 79.9 %all-gather = bf16[2048,192]{1,0:T(8,128)(2,1)S(1)} all-gather(bf16[64,192]{1,0:T(8,128)(2,1)} %param.31), channel_id=2, replica_groups=mesh['wide'=8,'narrow'=4] {'wide','narrow'}, dimensions={0}, use_global_device_ids=true | all-gather | bytes 811008 | tf_op jit(solution)/shard_map/all_gather | solution.py:140
  122.8 7.7 copy.107
  134.9 6.2 add_convert_fusion.2
  148.3 7.7 copy.109
  156.0 27.3 %all-gather.16.cloned.1.call-done = bf16[3072,192]{1,0:T(8,128)(2,1)} async-done(((bf16[96,192]{1,0:T(8,128)(2,1)}), bf16[3072,192]{1,0:T(8,128)(2,1)}) %all-gather.16.cloned.1.call-update) | async-done | bytes 1179664 | tf_op jit(solution)/shard_map/all_gather | solution.py:142
  201.3 7.7 copy.108
  209.4 255.0 %while.26 = (s32[]{:T(128)}, bf16[48,512,64]{1,2,0:T(8,128)(2,1)S(1)}, f32[48,512]{1,0:T(8,128)}, s32[48]{0:T(128)S(1)}, bf16[48,512,64]{2,1,0:T(8,128)(2,1)}, /...) while((s32[]{:T(128)}, bf16[48,512,64]{1,2,0:T(8,128)(2,1)S(1)}, ...), condition=%wide.region_3.4_spmd, body=%wide.region_0.3_spmd.sunk | while | flops 69206016 | bytes 3693681 | solution.py:184
  473.3 7.5 fusion.69
  493.7 8.2 reshape.353
  509.7 68.5 %multiply_convert_fusion.1 = (bf16[2048,3072]{1,0:T(8,128)(2,1)}, f32[2048,3072]{1,0:T(8,128)}, f32[2048,3072]{1,0:T(8,128)}) fusion(f32[3072]{0:T(1024)S(1)} %convert_element_type.206, bf16[768,3072]{1,0:T(8,128)(2,1)S(1)} %bitcast.362, f32[2048,768]{1,0:T(8,128)S(1)} %bitcast.331, f32[768]{0:T(1024)S(1)} %convert_element_type.204, ...), kind=kOutput, calls=%fused_computation.60 | convolution fusion | flops 10086776832 | bytes 73959424 | tf_op jit(solution)/shard_map/dot_general | solution.py:23
  578.3 15.1 fusion.70
  606.5 29.2 %convert_reduce_fusion = (f32[3072]{0:T(1024)}, bf16[2048,3072]{1,0:T(8,128)(2,1)}) fusion(f32[2048,3072]{1,0:T(8,128)} %get-tuple-element.196, bf16[2048,768]{1,0:T(8,128)(2,1)S(1)} %get-tuple-element.188, bf16[3072,768]{0,1:T(8,128)(2,1)} %bitcast.364, f32[2048,3072]{1,0:T(8,128)} %get-tuple-element.209, f32[3072]{0:T(1024)S(1)} %convert_element_type.206), kind=kOutput, calls=%fused_computation.58 | convolution fusion | flops 9770628096 | bytes 70803456 | tf_op jit(solution)/shard_map/dot_general | solution.py:33
  635.7 19.3 multiply_reduce_fusion.1
  675.8 7.7 copy.112
  687.9 467.8 %while.27 = (s32[]{:T(128)}, bf16[48,512,64]{1,2,0:T(8,128)(2,1)S(1)}, bf16[48,512,64]{1,2,0:T(8,128)(2,1)}, bf16[48,512,64]{1,2,0:T(8,128)(2,1)}, s32[48]{0:T(1...) while((s32[]{:T(128)}, ...), condition=%wide.region_14.15_spmd, body=%wide.region_12.14_spmd.sunk | while | flops 170196992 | bytes 9191553 | solution.py:238
  1177.7 9.6 select_reduce_fusion.1
  1191.6 8.0 fusion.76
  1220.8 8.0 fusion.73
  1228.9 7.9 fusion.74
  1236.9 8.0 fusion.75
  1245.0 16.6 fusion.77
  1273.5 18.5 fusion.61
  1292.0 12.6 reshape.367
  1304.6 9.0 copy.101
  1325.0 40.7 %all-reduce = (f32[2,768]{1,0:T(2,128)}, f32[768]{0:T(1024)}, f32[768]{0:T(1024)}, f32[768]{0:T(1024)}, f32[768]{0:T(1024)}, /*index=5*/f32[768]{0:T(1024)}, f32...) all-reduce(f32[2,768]{1,0:T(2,128)S(1)} %pad_maximum_fusion, ...), channel_id=1, replica_groups=mesh['wide'=8,'narrow'=4] {'wide','narrow'}, use_global_device_ids=true, to_apply=%region_19.20 | all-reduce | flops 10752 | bytes 86016 | tf_op jit(solution)/shard_map/psum | solution.py:326
  1365.8 61.1 %reduce-scatter.16.cloned.1.call-done = f32[1,96,192]{2,1,0:T(8,128)} async-done(((f32[32,96,192]{2,1,0:T(8,128)}), f32[1,96,192]{2,1,0:T(8,128)}) %reduce-scatter.16.cloned.1.call-update) | async-done | bytes 73744 | tf_op jit(solution)/shard_map/reduce_scatter | solution.py:303
  1426.8 142.2 %reduce-scatter.8.cloned.1.call-done = f32[1,64,192]{2,1,0:T(8,128)} async-done(((f32[32,64,192]{2,1,0:T(8,128)}), f32[1,64,192]{2,1,0:T(8,128)}) %reduce-scatter.8.cloned.1.call-update) | async-done | bytes 49168 | tf_op jit(solution)/shard_map/reduce_scatter | solution.py:279
  1569.0 105.6 %reduce-scatter.10.cloned.1.call-done = f32[1,96,192]{2,1,0:T(8,128)} async-done(((f32[32,96,192]{2,1,0:T(8,128)}), f32[1,96,192]{2,1,0:T(8,128)}) %reduce-scatter.10.cloned.1.call-update) | async-done | bytes 73744 | tf_op jit(solution)/shard_map/reduce_scatter | solution.py:285
  1674.6 107.3 %reduce-scatter.12.cloned.1.call-done = f32[1,96,192]{2,1,0:T(8,128)} async-done(((f32[32,96,192]{2,1,0:T(8,128)}), f32[1,96,192]{2,1,0:T(8,128)}) %reduce-scatter.12.cloned.1.call-update) | async-done | bytes 73744 | tf_op jit(solution)/shard_map/reduce_scatter | solution.py:291
  1781.9 107.1 %reduce-scatter.14.cloned.1.call-done = f32[1,96,192]{2,1,0:T(8,128)} async-done(((f32[32,96,192]{2,1,0:T(8,128)}), f32[1,96,192]{2,1,0:T(8,128)}) %reduce-scatter.14.cloned.1.call-update) | async-done | bytes 73744 | tf_op jit(solution)/shard_map/reduce_scatter | solution.py:297
  1889.0 141.7 %reduce-scatter.20.cloned.1.call-done = f32[1,384,192]{1,2,0:T(8,128)} async-done(((f32[32,384,192]{1,2,0:T(8,128)}), f32[1,384,192]{1,2,0:T(8,128)}) %reduce-scatter.20.cloned.1.call-update) | async-done | bytes 294928 | tf_op jit(solution)/shard_map/reduce_scatter | solution.py:318
  2030.7 141.5 %reduce-scatter.18.cloned.1.call-done = f32[1,96,768]{2,1,0:T(8,128)} async-done(((f32[32,96,768]{2,1,0:T(8,128)}), f32[1,96,768]{2,1,0:T(8,128)}) %reduce-scatter.18.cloned.1.call-update) | async-done | bytes 294928 | tf_op jit(solution)/shard_map/reduce_scatter | solution.py:312
  (1001 shorter events, 925.5 us)
Async XLA Ops:
  7.2 91.5 %copy-start = (bf16[100,768]{1,0:T(8,128)(2,1)S(1)}, bf16[100,768]{1,0:T(8,128)(2,1)}, u32[]{:S(2)}) copy-start(bf16[100,768]{1,0:T(8,128)(2,1)} %param.33) | copy-start | bytes 460804
  7.2 88.8 %copy-start.36 = (bf16[768]{0:T(1024)(128)(2,1)S(1)}, bf16[768]{0:T(1024)(128)(2,1)}, u32[]{:S(2)}) copy-start(bf16[768]{0:T(1024)(128)(2,1)} %param.38) | copy-start | bytes 4612
  7.2 88.8 %copy-start.37 = (bf16[768]{0:T(1024)(128)(2,1)S(1)}, bf16[768]{0:T(1024)(128)(2,1)}, u32[]{:S(2)}) copy-start(bf16[768]{0:T(1024)(128)(2,1)} %param.39) | copy-start | bytes 4612
  7.2 88.8 %copy-start.46 = (s32[4]{0:T(128)S(1)}, s32[4]{0:T(128)}, u32[]{:S(2)}) copy-start(s32[4]{0:T(128)} %param.28) | copy-start | bytes 52
  7.2 89.0 %copy-start.38 = (bf16[768]{0:T(1024)(128)(2,1)S(1)}, bf16[768]{0:T(1024)(128)(2,1)}, u32[]{:S(2)}) copy-start(bf16[768]{0:T(1024)(128)(2,1)} %param.40) | copy-start | bytes 4612
  7.2 89.0 %copy-start.39 = (bf16[768]{0:T(1024)(128)(2,1)S(1)}, bf16[768]{0:T(1024)(128)(2,1)}, u32[]{:S(2)}) copy-start(bf16[768]{0:T(1024)(128)(2,1)} %param.41) | copy-start | bytes 4612
  7.3 89.0 %copy-start.40 = (bf16[768]{0:T(1024)(128)(2,1)S(1)}, bf16[768]{0:T(1024)(128)(2,1)}, u32[]{:S(2)}) copy-start(bf16[768]{0:T(1024)(128)(2,1)} %param.42) | copy-start | bytes 4612
  7.3 89.0 %copy-start.30 = (bf16[3072]{0:T(1024)(128)(2,1)S(1)}, bf16[3072]{0:T(1024)(128)(2,1)}, u32[]{:S(2)}) copy-start(bf16[3072]{0:T(1024)(128)(2,1)} %param.44) | copy-start | bytes 18436
  7.3 89.0 %copy-start.41 = (bf16[768]{0:T(1024)(128)(2,1)S(1)}, bf16[768]{0:T(1024)(128)(2,1)}, u32[]{:S(2)}) copy-start(bf16[768]{0:T(1024)(128)(2,1)} %param.46) | copy-start | bytes 4612
  7.3 89.6 %copy-start.42 = (bf16[768]{0:T(1024)(128)(2,1)S(1)}, bf16[768]{0:T(1024)(128)(2,1)}, u32[]{:S(2)}) copy-start(bf16[768]{0:T(1024)(128)(2,1)} %param.47) | copy-start | bytes 4612
  7.3 90.2 %copy-start.43 = (bf16[768]{0:T(1024)(128)(2,1)S(1)}, bf16[768]{0:T(1024)(128)(2,1)}, u32[]{:S(2)}) copy-start(bf16[768]{0:T(1024)(128)(2,1)} %param.48) | copy-start | bytes 4612
  7.3 91.4 %copy-start.44 = (s32[4]{0:T(128)S(1)}, s32[4]{0:T(128)}, u32[]{:S(2)}) copy-start(s32[4]{0:T(128)} %param.30) | copy-start | bytes 52
  7.3 97.7 %all-gather.14.cloned.1.call-start = ((), (), s32[]{:S(2)}) async-start(), calls=%async_computation.15 | async-start | bytes 1622016 | tf_op jit(solution)/shard_map/all_gather | solution.py:141
  8.1 122.4 %all-gather.18.cloned.1.call-start = ((), (), s32[]{:S(2)}) async-start(), calls=%async_computation.17 | async-start | bytes 1622016 | tf_op jit(solution)/shard_map/all_gather | solution.py:143
  8.8 174.5 %all-gather.16.cloned.1.call-start = ((), (), s32[]{:S(2)}) async-start(), calls=%async_computation.16 | async-start | bytes 1622016 | tf_op jit(solution)/shard_map/all_gather | solution.py:142
  9.5 459.9 %all-gather.20.cloned.1.call-start = ((), (), s32[]{:S(2)}) async-start(), calls=%async_computation.18 | async-start | bytes 1622016 | tf_op jit(solution)/shard_map/all_gather | solution.py:144
  10.1 474.4 %all-gather.22.cloned.1.call-start = ((), (), s32[]{:S(2)}) async-start(), calls=%async_computation.19 | async-start | bytes 4866048 | tf_op jit(solution)/shard_map/all_gather | solution.py:150
  10.7 483.0 %all-gather.24.cloned.1.call-start = ((), (), s32[]{:S(2)}) async-start(), calls=%async_computation.20 | async-start | bytes 4866048 | tf_op jit(solution)/shard_map/all_gather | solution.py:151
  11.3 1354.5 %all-reduce.3.cloned.1.call-start = ((), (), s32[]{:S(2)}) async-start(), calls=%async_computation.8 | async-start | bytes 638976 | tf_op jit(solution)/shard_map/psum | solution.py:326
  96.3 482.0 %copy-start.33 = (f32[768]{0:T(1024)}, f32[768]{0:T(1024)S(1)}, u32[]{:S(2)}) copy-start(f32[768]{0:T(1024)S(1)} %convert_element_type.204) | copy-start | bytes 9220
  509.7 68.5 %copy-start.35 = (f32[768]{0:T(1024)S(1)}, f32[768]{0:T(1024)}, u32[]{:S(2)}) copy-start(f32[768]{0:T(1024)} %convert_element_type.208) | copy-start | bytes 9220
  606.5 29.2 %copy-start.12 = (bf16[2048,768]{1,0:T(8,128)(2,1)}, bf16[2048,768]{1,0:T(8,128)(2,1)S(1)}, u32[]{:S(2)}) copy-start(bf16[2048,768]{1,0:T(8,128)(2,1)S(1)} %get-tuple-element.188) | copy-start | bytes 9437188
  635.7 19.3 copy-start.22
  1166.4 11.3 slice-start
  1191.5 235.3 %reduce-scatter.16.cloned.1.call-start = ((), (), s32[]{:S(2)}) async-start(), calls=%async_computation.12 | async-start | bytes 3244032 | tf_op jit(solution)/shard_map/reduce_scatter | solution.py:303
  1199.6 369.5 %reduce-scatter.8.cloned.1.call-start = ((), (), s32[]{:S(2)}) async-start(), calls=%async_computation.7 | async-start | bytes 2162688 | tf_op jit(solution)/shard_map/reduce_scatter | solution.py:279
  1211.3 463.3 %reduce-scatter.10.cloned.1.call-start = ((), (), s32[]{:S(2)}) async-start(), calls=%async_computation.9 | async-start | bytes 3244032 | tf_op jit(solution)/shard_map/reduce_scatter | solution.py:285
  1228.9 553.0 %reduce-scatter.12.cloned.1.call-start = ((), (), s32[]{:S(2)}) async-start(), calls=%async_computation.10 | async-start | bytes 3244032 | tf_op jit(solution)/shard_map/reduce_scatter | solution.py:291
  1236.9 652.1 %reduce-scatter.14.cloned.1.call-start = ((), (), s32[]{:S(2)}) async-start(), calls=%async_computation.11 | async-start | bytes 3244032 | tf_op jit(solution)/shard_map/reduce_scatter | solution.py:297
  1244.9 785.8 %reduce-scatter.20.cloned.1.call-start = ((), (), s32[]{:S(2)}) async-start(), calls=%async_computation.14 | async-start | bytes 9732096 | tf_op jit(solution)/shard_map/reduce_scatter | solution.py:318
  1272.8 899.4 %reduce-scatter.18.cloned.1.call-start = ((), (), s32[]{:S(2)}) async-start(), calls=%async_computation.13 | async-start | bytes 9732096 | tf_op jit(solution)/shard_map/reduce_scatter | solution.py:312
  1313.7 860.2 %copy-start.1 = (bf16[100,768]{1,0:T(8,128)(2,1)S(1)}, bf16[100,768]{1,0:T(8,128)(2,1)}, u32[]{:S(2)}) copy-start(bf16[100,768]{1,0:T(8,128)(2,1)} %param.33) | copy-start | bytes 460804
  (35 other events, 192.2 us)
Sparse Core Ops, SparseCore 0:
  11.0 58.6 all-gather.13
  72.6 53.8 all-gather.17
  129.4 53.8 all-gather.15
  186.0 53.9 all-gather.19
  242.7 62.4 all-gather.21
  308.0 62.0 all-gather.23
  1191.6 126.0 all-reduce.2
  1323.7 103.1 reduce-scatter.15
  1429.7 139.3 reduce-scatter.7
  1574.9 99.7 reduce-scatter.9
  1680.7 101.1 reduce-scatter.11
  1787.8 101.2 reduce-scatter.13
  1895.5 135.1 reduce-scatter.19
  2037.0 135.1 reduce-scatter.17
where the time goes:
time: 2200 us; the launch traced here: 2180 us
  waiting for transfers between devices  838 us (38%)
  matrix products  730 us (33%)
  local copies, waits for them, and re-layouts  344 us (16%)
  other arithmetic  131 us (6%)
  blocking collectives  121 us (6%)
    dot_general x150, matrix products, matmul_second_t(): lax.dot_general(left_side, right_side, (((1,), (1,)), ((), ())), preferre...  262 us
    dot_general x102, matrix products, matmul_first_t(): lax.dot_general(left_side, right_side, (((0,), (0,)), ((), ())), preferre...  243 us
    dot_general x103, matrix products, matmul(): return jnp.dot(left_side, right_side, preferred_element_type=jnp.float32)  224 us
    reduce_scatter x1, waiting for transfers between devices, on_device(): lax.psum_scatter(disassemble(position_local, wide_count, narrow_count), (...  142 us
    reduce_scatter x1, waiting for transfers between devices, on_device(): lax.psum_scatter(disassemble(down_weight_grad, wide_count, narrow_count),...  142 us
    reduce_scatter x1, waiting for transfers between devices, on_device(): lax.psum_scatter(disassemble(up_weight_grad, wide_count, narrow_count), (...  141 us
    reduce_scatter x1, waiting for transfers between devices, on_device(): lax.psum_scatter(disassemble(key_weight_grad, wide_count, narrow_count),...  107 us
    reduce_scatter x1, waiting for transfers between devices, on_device(): lax.psum_scatter(disassemble(value_weight_grad, wide_count, narrow_count)...  107 us
  transfers between devices with their start and end apart: 14, of which 8 were waited for; matrix products, arithmetic and copies ran while one was open for 23% of the time, Pallas kernels for 0%

commit v1 on v0

v1 whole, which is shorter than its diff:
```python
import math

import jax
import jax.numpy as jnp
from jax import lax
from jax.experimental import pallas as pl
from jax.experimental.pallas import tpu as pltpu
from jax.sharding import PartitionSpec as P

H = 12
HD = 64
EPSILON = 1e-05
NEG = -1e30


def normalize(inputs, scales, offset):
    average = jnp.mean(inputs, axis=-1, keepdims=True)
    centered = inputs - average
    spread = jnp.mean(centered * centered, axis=-1, keepdims=True)
    return centered * lax.rsqrt(spread + EPSILON) * scales + offset


def matmul(left_side, right_side):
    return jnp.dot(left_side, right_side, preferred_element_type=jnp.float32)


def matmul_first_t(left_side, right_side):
    return lax.dot_general(
        left_side, right_side, (((0,), (0,)), ((), ())), preferred_element_type=jnp.float32
    )


def matmul_second_t(left_side, right_side):
    return lax.dot_general(
        left_side, right_side, (((1,), (1,)), ((), ())), preferred_element_type=jnp.float32
    )


def exact_gelu(inputs):
    return jax.nn.gelu(inputs, approximate=False)


LANES = 384


def swap_partners(values, axis_name, mask):
    count = lax.axis_size(axis_name)
    return lax.ppermute(values, axis_name, [(i, i ^ mask) for i in range(count)])


def fold(shard):
    rows, cols = shard.shape
    if cols >= LANES:
        parts = cols // LANES
        return shard.reshape(rows, parts, LANES).transpose(1, 0, 2).reshape(rows * parts, LANES)
    parts = LANES // cols
    return shard.reshape(parts, rows // parts, cols).transpose(1, 0, 2).reshape(-1, LANES)


def unfold(folded, rows, cols):
    if cols >= LANES:
        parts = cols // LANES
        return folded.reshape(parts, rows, LANES).transpose(1, 0, 2).reshape(rows, cols)
    parts = LANES // cols
    return folded.reshape(-1, parts, cols).transpose(1, 0, 2).reshape(rows, cols)


def gather_pieces(folded):
    narrow_count = lax.axis_size("narrow")
    wide_count = lax.axis_size("wide")
    column = jnp.stack(
        [folded] + [swap_partners(folded, "narrow", k) for k in range(1, narrow_count)]
    )
    chips = [column] + [swap_partners(column, "wide", 2 * k) for k in range(1, wide_count // 2)]
    pieces = []
    for piece in chips:
        pieces += [piece, swap_partners(piece, "wide", 1)]
    return pieces


def scatter_sum(kept, sent):
    narrow_count = lax.axis_size("narrow")
    chip_count = lax.axis_size("wide") // 2
    wide32 = lambda values: values.astype(jnp.float32)
    arrived = swap_partners(sent, "wide", 1)
    sums = [
        (wide32(kept[k]) + wide32(arrived[k])).astype(jnp.bfloat16) for k in range(chip_count)
    ]
    total = wide32(sums[0])
    for k in range(1, chip_count):
        total = total + wide32(swap_partners(sums[k], "wide", 2 * k))
    total = total.astype(jnp.bfloat16)
    result = wide32(total[0])
    for k in range(1, narrow_count):
        result = result + wide32(swap_partners(total[k], "narrow", k))
    return result


def dot_nt(a,b): return lax.dot_general(a,b,(((1,),(1,)),((),())),preferred_element_type=jnp.float32)
def dot_nn(a,b): return lax.dot_general(a,b,(((1,),(0,)),((),())),preferred_element_type=jnp.float32)

def head_half(x, which):
    lane=lax.broadcasted_iota(jnp.int32,x.shape,1)
    keep=(lane<HD) if which==0 else (lane>=HD)
    return jnp.where(keep,x,jnp.zeros_like(x))

def mask_tail(s, live, length, fill):
    lo=s.shape[0]-128
    tail=s[lo:]
    key=lo+lax.broadcasted_iota(jnp.int32,tail.shape,0)
    tail=jnp.where(key<length,tail,fill)
    return tail if lo==0 else jnp.concatenate([s[:lo],tail],axis=0)

def fwd_kernel(len_ref,q_ref,k_ref,v_ref,o_ref,lse_ref):
    length=len_ref[pl.program_id(0)]
    nb=(length+127)//128
    seq=q_ref.shape[0]
    def run(live):
        k=k_ref[:live,:]
        vt=v_ref[:live,:].T
        q=q_ref[...]*jnp.bfloat16(0.125)
        outs=[];lses=[]
        for h in (0,1):
            s=dot_nt(k,head_half(q,h))
            s=mask_tail(s,live,length,NEG)
            m=jnp.max(s,axis=0,keepdims=True)
            p=jnp.exp(s-m)
            l=jnp.sum(p,axis=0,keepdims=True)
            low=(p*(1.0/l)).astype(jnp.bfloat16)
            outs.append(dot_nn(vt[h*HD:(h+1)*HD],low))
            lses.append(m+jnp.log(l))
        o_ref[...]=jnp.concatenate(outs,axis=0).T.astype(o_ref.dtype)
        lse_ref[...]=jnp.concatenate(lses,axis=0).reshape(lse_ref.shape)
    for j in range(1,seq//128+1):
        @pl.when(nb==j)
        def _(): run(j*128)

def bwd_kernel(len_ref,q_ref,k_ref,v_ref,do_ref,lse_ref,dq_ref,dk_ref,dv_ref):
    length=len_ref[pl.program_id(0)]
    nb=(length+127)//128
    seq=q_ref.shape[0]
    def run(live):
        k=k_ref[:live,:]
        v=v_ref[:live,:]
        kt=k.T
        q=q_ref[...]*jnp.bfloat16(0.125)
        do=do_ref[...]
        lse=lse_ref[...].reshape(2,seq)
        dk=None;dv=None;dqs=[]
        for h in (0,1):
            qh=head_half(q,h); doh=head_half(do,h)
            s=dot_nt(k,qh)
            s=mask_tail(s,live,length,NEG)
            p=jnp.exp(s-lse[h:h+1])
            dp=dot_nt(v,doh)
            delta=jnp.sum(p*dp,axis=0,keepdims=True)
            ds=(p*(dp-delta)).astype(jnp.bfloat16)
            low=p.astype(jnp.bfloat16)
            a=dot_nn(low,doh); b=dot_nn(ds,qh)
            dv=a if dv is None else dv+a
            dk=b if dk is None else dk+b
            dqs.append(dot_nn(kt[h*HD:(h+1)*HD],ds))
        dq_ref[...]=(jnp.concatenate(dqs,axis=0).T*0.125).astype(dq_ref.dtype)
        dk_ref[:live,:]=dk.astype(dk_ref.dtype)
        dv_ref[:live,:]=dv.astype(dv_ref.dtype)
        if live<seq:
            dk_ref[live:,:]=jnp.zeros((seq-live,128),dk_ref.dtype)
            dv_ref[live:,:]=jnp.zeros((seq-live,128),dv_ref.dtype)
    for j in range(1,seq//128+1):
        @pl.when(nb==j)
        def _(): run(j*128)

def attention_forward(lengths,q,k,v,pairs,seq):
    groups=q.shape[1]//128
    spec=pl.BlockSpec((seq,128),lambda b,g,n:(b,g))
    lspec=pl.BlockSpec((1,1,2,seq),lambda b,g,n:(b,g,0,0))
    return pl.pallas_call(fwd_kernel,
        grid_spec=pltpu.PrefetchScalarGridSpec(num_scalar_prefetch=1,grid=(pairs,groups),
            in_specs=[spec,spec,spec],out_specs=[spec,lspec]),
        out_shape=[jax.ShapeDtypeStruct(q.shape,jnp.bfloat16),jax.ShapeDtypeStruct((pairs,groups,2,seq),jnp.float32)],
        name='attention_forward',
    )(lengths,q,k,v)

def attention_backward(lengths,q,k,v,do,lse,pairs,seq):
    groups=q.shape[1]//128
    spec=pl.BlockSpec((seq,128),lambda b,g,n:(b,g))
    lspec=pl.BlockSpec((1,1,2,seq),lambda b,g,n:(b,g,0,0))
    return pl.pallas_call(bwd_kernel,
        grid_spec=pltpu.PrefetchScalarGridSpec(num_scalar_prefetch=1,grid=(pairs,groups),
            in_specs=[spec,spec,spec,spec,lspec],out_specs=[spec,spec,spec]),
        out_shape=[jax.ShapeDtypeStruct(q.shape,jnp.bfloat16)]*3,
        name='attention_backward',
    )(lengths,q,k,v,do,lse)


def on_device(
    tokens,
    lengths,
    query_lengths,
    language_ids,
    position_table,
    segment_table,
    language_table,
    query_weight,
    key_weight,
    value_weight,
    output_weight,
    query_bias,
    value_bias,
    output_bias,
    first_gain,
    first_shift,
    up_weight,
    up_bias,
    down_weight,
    down_bias,
    second_gain,
    second_shift,
    cotangent,
):
    seq_count, seq_len, features = tokens.shape
    row_count = seq_count * seq_len
    wide_count = lax.axis_size("wide")
    narrow_count = lax.axis_size("narrow")
    me_wide = lax.axis_index("wide")
    me_narrow = lax.axis_index("narrow")
    wide_order = lax.iota(jnp.int32, wide_count) ^ me_wide
    narrow_order = lax.iota(jnp.int32, narrow_count) ^ me_narrow

    def assembled(pieces, first_row, rows, cols):
        folded_rows = rows * cols // LANES
        stacked = jnp.stack([piece[:, first_row : first_row + folded_rows] for piece in pieces])
        stacked = jnp.take(jnp.take(stacked, wide_order, axis=0), narrow_order, axis=1)
        if cols >= LANES:
            blocks = stacked.reshape(wide_count, narrow_count, cols // LANES, rows, LANES)
            return blocks.transpose(0, 3, 1, 2, 4).reshape(wide_count * rows, narrow_count * cols)
        parts = LANES // cols
        blocks = stacked.reshape(wide_count, narrow_count, rows // parts, parts, cols)
        return blocks.transpose(0, 3, 2, 1, 4).reshape(wide_count * rows, narrow_count * cols)

    def assembled_down(pieces, first_row, rows, cols):
        folded_rows = rows * cols // LANES
        stacked = jnp.stack([piece[:, first_row : first_row + folded_rows] for piece in pieces])
        stacked = jnp.take(jnp.take(stacked, wide_order, axis=0), narrow_order, axis=1)
        if cols >= LANES:
            blocks = stacked.reshape(wide_count, narrow_count, cols // LANES, rows, LANES)
            return blocks.transpose(1, 3, 0, 2, 4).reshape(narrow_count * rows, wide_count * cols)
        parts = LANES // cols
        blocks = stacked.reshape(wide_count, narrow_count, rows // parts, parts, cols)
        return blocks.transpose(1, 3, 2, 0, 4).reshape(narrow_count * rows, wide_count * cols)

    def split_up(whole, rows, cols, transposed=False):
        whole = whole.astype(jnp.bfloat16)
        if cols >= LANES:
            if transposed:
                blocks = whole.reshape(narrow_count, rows, wide_count, cols // LANES, LANES)
                blocks = blocks.transpose(2, 0, 3, 1, 4)
            else:
                blocks = whole.reshape(wide_count, rows, narrow_count, cols // LANES, LANES)
                blocks = blocks.transpose(0, 2, 3, 1, 4)
        else:
            parts = LANES // cols
            if transposed:
                blocks = whole.reshape(narrow_count, parts, rows // parts, wide_count, cols)
                blocks = blocks.transpose(3, 0, 2, 1, 4)
            else:
                blocks = whole.reshape(wide_count, parts, rows // parts, narrow_count, cols)
                blocks = blocks.transpose(0, 3, 2, 1, 4)
        blocks = blocks.reshape(wide_count, narrow_count, rows * cols // LANES, LANES)
        return jnp.take(jnp.take(blocks, wide_order, axis=0), narrow_order, axis=1)

    def owner_sums(blocks):
        joined = jnp.concatenate(blocks, axis=2)
        chips = joined.reshape((wide_count // 2, 2) + joined.shape[1:])
        return scatter_sum(chips[:, 0], chips[:, 1])

    def shard_of(sums, first_row, rows, cols):
        return unfold(sums[first_row : first_row + rows * cols // LANES], rows, cols)

    position_rows, position_cols = position_table.shape
    weight_rows, weight_cols = query_weight.shape
    up_rows, up_cols = up_weight.shape
    down_rows, down_cols = down_weight.shape
    position_fold = position_rows * position_cols // LANES
    weight_fold = weight_rows * weight_cols // LANES
    up_fold = up_rows * up_cols // LANES
    down_fold = down_rows * down_cols // LANES

    first_pieces = gather_pieces(
        jnp.concatenate(
            [fold(position_table), fold(query_weight), fold(key_weight), fold(value_weight)]
        )
    )
    later_pieces = gather_pieces(
        jnp.concatenate([fold(up_weight), fold(down_weight.T), fold(output_weight)])
    )
    position_full = assembled(first_pieces, 0, position_rows, position_cols)
    query_full, key_full, value_full = [
        assembled(first_pieces, position_fold + i * weight_fold, weight_rows, weight_cols)
        for i in range(3)
    ]
    up_full = assembled(later_pieces, 0, up_rows, up_cols)
    down_across = assembled_down(later_pieces, up_fold, down_cols, down_rows)
    output_full = assembled(later_pieces, up_fold + down_fold, weight_rows, weight_cols)
    places = lax.broadcasted_iota(jnp.int32, (seq_count, seq_len), 1)
    passage = (places >= query_lengths[:, None])[:, :, None]
    segment_float = segment_table.astype(jnp.float32)
    segment_rows = jnp.where(passage, segment_float[1], segment_float[0])
    language_count = language_table.shape[0]
    language_hot = (
        language_ids[:, None] == lax.broadcasted_iota(jnp.int32, (seq_count, language_count), 1)
    ).astype(jnp.bfloat16)
    language_rows = matmul(language_hot, language_table)
    start = (
        tokens.astype(jnp.float32)
        + position_full.astype(jnp.float32)[None]
        + segment_rows
        + language_rows[:, None, :]
    )
    flattened = start.reshape(row_count, features)
    first_in = flattened.astype(jnp.bfloat16)
    query_rows = (matmul(first_in, query_full) + query_bias.astype(jnp.float32)).astype(
        jnp.bfloat16
    )
    key_rows = matmul(first_in, key_full).astype(jnp.bfloat16)
    value_rows = (matmul(first_in, value_full) + value_bias.astype(jnp.float32)).astype(
        jnp.bfloat16
    )
    context, log_totals = attention_forward(
        lengths, query_rows, key_rows, value_rows, seq_count, seq_len
    )
    attended = matmul(context, output_full) + output_bias.astype(jnp.float32)
    first_out, first_pull = jax.vjp(
        normalize,
        flattened + attended,
        first_gain.astype(jnp.float32),
        first_shift.astype(jnp.float32),
    )
    second_in = first_out.astype(jnp.bfloat16)
    hidden_pre = matmul(second_in, up_full) + up_bias.astype(jnp.float32)
    hidden = exact_gelu(hidden_pre).astype(jnp.bfloat16)
    branch = matmul_second_t(hidden, down_across) + down_bias.astype(jnp.float32)
    final, second_pull = jax.vjp(
        normalize,
        first_out + branch,
        second_gain.astype(jnp.float32),
        second_shift.astype(jnp.float32),
    )
    layer_out = final.astype(jnp.bfloat16).reshape(seq_count, seq_len, features)
    grad_second, second_gain_grad, second_shift_grad = second_pull(
        cotangent.astype(jnp.float32).reshape(row_count, features)
    )
    grad_branch = grad_second.astype(jnp.bfloat16)
    down_bias_grad = jnp.sum(grad_branch.astype(jnp.float32), axis=0)
    down_across_grad = matmul_first_t(grad_branch, hidden)
    gelu_value, gelu_pull = jax.vjp(exact_gelu, hidden_pre)
    grad_hidden = gelu_pull(matmul(grad_branch, down_across))[0].astype(jnp.bfloat16)
    up_bias_grad = jnp.sum(grad_hidden.astype(jnp.float32), axis=0)
    up_weight_grad = matmul_first_t(second_in, grad_hidden)
    forward_sums = owner_sums(
        [
            split_up(up_weight_grad, up_rows, up_cols),
            split_up(down_across_grad, down_cols, down_rows, True),
        ]
    )
    grad_first_out = grad_second + matmul_second_t(grad_hidden, up_full)
    grad_first, first_gain_grad, first_shift_grad = first_pull(grad_first_out)
    grad_attended = grad_first.astype(jnp.bfloat16)
    output_bias_grad = jnp.sum(grad_attended.astype(jnp.float32), axis=0)
    output_weight_grad = matmul_first_t(context, grad_attended)
    grad_context = matmul_second_t(grad_attended, output_full).astype(jnp.bfloat16)
    grad_query, grad_key, grad_value = attention_backward(
        lengths, query_rows, key_rows, value_rows, grad_context, log_totals, seq_count, seq_len
    )
    query_bias_grad = jnp.sum(grad_query.astype(jnp.float32), axis=0)
    value_bias_grad = jnp.sum(grad_value.astype(jnp.float32), axis=0)
    query_weight_grad = matmul_first_t(first_in, grad_query)
    key_weight_grad = matmul_first_t(first_in, grad_key)
    value_weight_grad = matmul_first_t(first_in, grad_value)
    grad_start = (
        grad_first
        + matmul_second_t(grad_query, query_full)
        + matmul_second_t(grad_key, key_full)
        + matmul_second_t(grad_value, value_full)
    )
    token_grad = grad_start.astype(jnp.bfloat16).reshape(seq_count, seq_len, features)
    grad_start_pairs = grad_start.reshape(seq_count, seq_len, features)
    position_local = jnp.sum(grad_start_pairs, axis=0)
    segment_local = jnp.stack(
        [
            jnp.sum(jnp.where(passage, 0.0, grad_start_pairs), axis=(0, 1)),
            jnp.sum(jnp.where(passage, grad_start_pairs, 0.0), axis=(0, 1)),
        ]
    )
    attention_sums = owner_sums(
        [split_up(position_local, position_rows, position_cols)]
        + [
            split_up(grad, weight_rows, weight_cols)
            for grad in (query_weight_grad, key_weight_grad, value_weight_grad, output_weight_grad)
        ]
    )
    small = jnp.concatenate(
        [
            jnp.sum(grad_start_pairs, axis=1),
            jnp.broadcast_to(language_ids.astype(jnp.float32)[:, None], (seq_count, features)),
            segment_local,
            query_bias_grad[None],
            value_bias_grad[None],
            output_bias_grad[None],
            first_gain_grad[None],
            first_shift_grad[None],
            down_bias_grad[None],
            second_gain_grad[None],
            second_shift_grad[None],
            up_bias_grad.reshape(-1, features),
        ]
    )
    everyone = jnp.stack(gather_pieces(small))
    everyone = jnp.take(jnp.take(everyone, wide_order, axis=0), narrow_order, axis=1)
    everyone = everyone.reshape((wide_count * narrow_count,) + small.shape)
    pair_sums = everyone[:, :seq_count].reshape(-1, features)
    pair_ids = everyone[:, seq_count : 2 * seq_count, 0].reshape(-1).astype(jnp.int32)
    small_sums = jnp.sum(everyone[:, 2 * seq_count :], axis=0)
    language_count_all = lax.broadcasted_iota(jnp.int32, (language_count, pair_ids.shape[0]), 0)
    language_sums = jnp.dot(
        (language_count_all == pair_ids[None]).astype(jnp.float32),
        pair_sums,
        precision=lax.Precision.HIGHEST,
    )
    weight_sums = [
        shard_of(attention_sums, position_fold + i * weight_fold, weight_rows, weight_cols)
        for i in range(4)
    ]
    return (
        layer_out,
        token_grad,
        shard_of(attention_sums, 0, position_rows, position_cols),
        small_sums[:2],
        language_sums,
        weight_sums[0],
        weight_sums[1],
        weight_sums[2],
        weight_sums[3],
        small_sums[2],
        small_sums[3],
        small_sums[4],
        small_sums[5],
        small_sums[6],
        shard_of(forward_sums, 0, up_rows, up_cols),
        small_sums[10:].reshape(-1),
        shard_of(forward_sums, up_fold, down_cols, down_rows).T,
        small_sums[7],
        small_sums[8],
        small_sums[9],
    )


def solution(mesh):
    return jax.shard_map(
        on_device,
        mesh=mesh,
        in_specs=(
            P(("wide", "narrow"), None, None),
            P(("wide", "narrow")),
            P(("wide", "narrow")),
            P(("wide", "narrow")),
            P("wide", "narrow"),
            P(),
            P(),
            P("wide", "narrow"),
            P("wide", "narrow"),
            P("wide", "narrow"),
            P("wide", "narrow"),
            P(),
            P(),
            P(),
            P(),
            P(),
            P("wide", "narrow"),
            P(),
            P("wide", "narrow"),
            P(),
            P(),
            P(),
            P(("wide", "narrow"), None, None),
        ),
        out_specs=(
            P(("wide", "narrow"), None, None),
            P(("wide", "narrow"), None, None),
            P("wide", "narrow"),
            P(),
            P(),
            P("wide", "narrow"),
            P("wide", "narrow"),
            P("wide", "narrow"),
            P("wide", "narrow"),
            P(),
            P(),
            P(),
            P(),
            P(),
            P("wide", "narrow"),
            P(),
            P("wide", "narrow"),
            P(),
            P(),
            P(),
        ),
        check_vma=False,
    )
```

time: 2200 us -> 910 us (0.41)
  waiting for transfers between devices: 838 us -> 128 us
  matrix products: 730 us -> 226 us
  blocking collectives: 121 us -> 0 us
  Pallas kernels: 0 us -> 64.8 us
  starting transfers between devices: 0.56 us -> 65.1 us
  local copies, waits for them, and re-layouts: 344 us -> 302 us
    reduce_scatter x7 -> x0, waiting for transfers between devices: 806 us -> none  [the longest x1 142 us: on_device(): lax.psum_scatter(disassemble(position_local, wide_count, narrow_count), (...]
    dot_general x150 -> x6, matrix products: 262 us -> 60 us  [matmul_second_t(): lax.dot_general(left_side, right_side, (((1,), (1,)), ((), ())), preferre...]
    dot_general x102 -> x6, matrix products: 243 us -> 46.6 us  [matmul_first_t(): lax.dot_general(left_side, right_side, (((0,), (0,)), ((), ())), preferre...]
    ppermute x0 -> x44, waiting for transfers between devices: none -> 128 us  [swap_partners(): lax.ppermute(values, axis_name, [(i, i ^ mask) for i in range(count)])]
    dot_general x103 -> x7, matrix products: 224 us -> 118 us  [matmul(): return jnp.dot(left_side, right_side, preferred_element_type=jnp.float32)]
    gather x0 -> x33, local copies, waits for them, and re-layouts: none -> 104 us  [the longest x14 41.5 us: split_up(): return jnp.take(jnp.take(blocks, wide_order, axis=0), narrow_order, axis=1)]
    dynamic_slice x144 -> x0, local copies, waits for them, and re-layouts: 90.9 us -> none  [the longest x96 55.9 us: on_device(): lax.map(attend_block, (query_heads, key_heads, value_heads, head_lengths))]
    all_gather x1 -> x0, blocking collectives: 79.9 us -> none  [on_device(): lax.all_gather(position_table[None], ('wide', 'narrow'), axis=0, tiled=True)]
  transfers between devices with their start and end apart: 14 -> 44, of which waited for: 8 -> 13; matrix products, arithmetic and copies ran while one was open for 23% -> 29% of each run, Pallas kernels for 0% -> 0%
where the time goes in v1:
time: 910 us; the launch traced here: 901 us
  local copies, waits for them, and re-layouts  302 us (33%)
  matrix products  226 us (25%)
  waiting for transfers between devices  128 us (14%)
  other arithmetic  113 us (12%)
  starting transfers between devices  65.1 us (7%)
  Pallas kernels  64.8 us (7%)
    ppermute x44, waiting for transfers between devices, swap_partners(): lax.ppermute(values, axis_name, [(i, i ^ mask) for i in range(count)])  128 us
    dot_general x7, matrix products, matmul(): return jnp.dot(left_side, right_side, preferred_element_type=jnp.float32)  118 us
    ppermute x44, starting transfers between devices, swap_partners(): lax.ppermute(values, axis_name, [(i, i ^ mask) for i in range(count)])  65.1 us
    unnamed x225, local copies, waits for them, and re-layouts  62.9 us
    dot_general x6, matrix products, matmul_second_t(): lax.dot_general(left_side, right_side, (((1,), (1,)), ((), ())), preferre...  60 us
    dot_general x6, matrix products, matmul_first_t(): lax.dot_general(left_side, right_side, (((0,), (0,)), ((), ())), preferre...  46.6 us
    gather x14, local copies, waits for them, and re-layouts, split_up(): return jnp.take(jnp.take(blocks, wide_order, axis=0), narrow_order, axis=1)  41.5 us
    pallas_call x1, Pallas kernels, attention_backward(): pl.pallas_call(bwd_kernel, grid_spec=pltpu.PrefetchScalarGridSpec(num_sca...  36.6 us
  transfers between devices with their start and end apart: 44, of which 13 were waited for; matrix products, arithmetic and copies ran while one was open for 29% of the time, Pallas kernels for 0%

profile of v1, /device:TPU:0, one launch (start us, length us, event | category | flops | bytes accessed | tf_op | source)
XLA Modules:
  0.0 901.2 jit_solution(9873094677297436585)
XLA Ops:
  33.5 9.9 %collective-permute-done.11 = bf16[432,384]{1,0:T(8,128)(2,1)} collective-permute-done((bf16[432,384]{1,0:T(8,128)(2,1)S(1)}, bf16[432,384]{1,0:T(8,128)(2,1)}, u32[]{:S(2)}, u32[]{:S(2)}) %collective-permute-start.11) | collective-permute-done | bytes 331808 | tf_op jit(solution)/shard_map/ppermute | solution.py:48
  95.6 19.1 %collective-permute-done.16 = bf16[4,432,384]{2,1,0:T(8,128)(2,1)} collective-permute-done((bf16[4,432,384]{2,1,0:T(8,128)(2,1)}, bf16[4,432,384]{2,1,0:T(8,128)(2,1)}, u32[]{:S(2)}, u32[]{:S(2)}) %collective-permute-start.16) | collective-permute-done | bytes 1327136 | tf_op jit(solution)/shard_map/ppermute | solution.py:48
  178.5 6.9 convolution_convert_fusion.3.k_ref
  193.3 28.2 %attention_forward.1 = (bf16[2048,768]{1,0:T(8,128)(2,1)}, f32[4,6,2,512]{3,2,1,0:T(2,128)}) custom-call(s32[4]{0:T(128)} %len_ref.3, bf16[2048,768]{1,0:T(8,128)(2,1)} %add_convert_fusion.3.q_ref, bf16[2048,768]{1,0:T(8,128)(2,1)} %convolution_convert_fusion.3.k_ref, bf16[2048,768]{1,0:T(8,128)(2,1)} %add_convert_fusion.2.v_ref), custom_call_target="tpu_custom_call" | custom-call | tf_op jit(solution)/shard_map/attention_forward/pallas_call | solution.py:177
  221.5 6.8 fusion.57
  252.0 8.4 broadcast_select_fusion.4
  266.1 5.8 gather_fusion.15
  271.8 8.5 select_bitcast_fusion.2
  280.3 8.7 copy.297
  289.0 11.3 %reshape.495 = bf16[768,3072]{1,0:T(8,128)(2,1)} reshape(bf16[8,96,4,2,384]{4,3,2,1,0:T(2,128)(2,1)} %bitcast.600) | data formatting | bytes 9437184 | tf_op jit(solution)/shard_map/reshape | solution.py:236
  310.2 68.6 %multiply_convert_fusion = (bf16[2048,3072]{1,0:T(8,128)(2,1)}, f32[2048,3072]{1,0:T(8,128)}, f32[2048,3072]{1,0:T(8,128)}) fusion(f32[3072]{0:T(1024)S(1)} %convert_element_type.347, bf16[768,3072]{1,0:T(8,128)(2,1)S(1)} %copy-done.15, f32[2048,768]{1,0:T(8,128)S(1)} %bitcast.597, f32[768]{0:T(1024)S(1)} %convert_element_type.345, ...), kind=kOutput, calls=%fused_computation.34 | convolution fusion | flops 10086776832 | bytes 73959424 | tf_op jit(solution)/shard_map/dot_general | solution.py:24
  378.8 15.5 %fusion.58 = (f32[2048]{0:T(1024)S(1)}, f32[2048,768]{1,0:T(8,128)S(1)}) fusion(f32[768]{0:T(1024)S(1)} %copy-done.66, bf16[2048,3072]{1,0:T(8,128)(2,1)} %get-tuple-element.101, bf16[768,3072]{1,0:T(8,128)(2,1)} %bitcast.622, f32[768]{0:T(1024)S(1)} %convert_element_type.345, f32[768]{0:T(1024)S(1)} %convert_element_type.344, f32[2048]{0:T(1024)S(1)} %fusion.41, ...), kind=kOutput, calls=%fused_computation.364 | convolution fusion | flops 9674684416 | bytes 29918208 | tf_op jit(solution)/shard_map/dot_general | solution.py:34
  407.6 11.7 %convolution_convert_fusion = bf16[768,3072]{1,0:T(8,128)(2,1)} fusion(bf16[2048,768]{1,0:T(8,128)(2,1)S(1)} %get-tuple-element.94, bf16[2048,3072]{1,0:T(8,128)(2,1)S(1)} %bitcast.666), kind=kOutput, calls=%fused_computation.82 | convolution fusion | flops 9666035712 | bytes 20447232 | tf_op jit(solution)/shard_map/dot_general | solution.py:28
  419.4 27.9 %convert_reduce_fusion = (f32[3072]{0:T(1024)S(1)}, bf16[2048,3072]{1,0:T(8,128)(2,1)}) fusion(f32[2048,3072]{1,0:T(8,128)} %get-tuple-element.102, bf16[2048,768]{1,0:T(8,128)(2,1)S(1)} %get-tuple-element.94, bf16[768,3072]{1,0:T(8,128)(2,1)} %bitcast.623, f32[2048,3072]{1,0:T(8,128)} %get-tuple-element.191, f32[3072]{0:T(1024)S(1)} %convert_element_type.347), kind=kOutput, calls=%fused_computation.32 | convolution fusion | flops 9770628096 | bytes 70803456 | tf_op jit(solution)/shard_map/dot_general | solution.py:24
  447.2 18.0 %convolution_convert_fusion.1 = bf16[768,3072]{1,0:T(8,128)(2,1)} fusion(bf16[2048,3072]{1,0:T(8,128)(2,1)} %get-tuple-element.197, f32[2048,768]{1,0:T(8,128)} %copy-done.9, f32[768]{0:T(1024)S(1)} %convert_element_type.345, f32[768]{0:T(1024)S(1)} %convert_element_type.344, f32[2048]{0:T(1024)S(1)} %fusion.41, f32[2048]{0:T(1024)S(1)} %broadcast_multiply_fusion.1), kind=kOutput, calls=%fused_computation.83 | convolution fusion | flops 9673900032 | bytes 23615488 | tf_op jit(solution)/shard_map/dot_general | solution.py:28
  465.3 20.4 %multiply_reduce_fusion = (f32[768]{0:T(1024)S(1)}, f32[2048]{0:T(1024)S(1)}, f32[768]{0:T(1024)S(1)}, f32[2048,768]{1,0:T(8,128)}) fusion(f32[2048,768]{1,0:T(8,128)} %copy-done.9, f32[2048]{0:T(1024)S(1)} %fusion.41, f32[2048]{0:T(1024)S(1)} %broadcast_multiply_fusion.1, f32[768]{0:T(1024)S(1)} %convert_element_type.344, ...), kind=kOutput, calls=%fused_computation.62 | convolution fusion | flops 9679400960 | bytes 36217856 | tf_op jit(solution)/shard_map/dot_general | solution.py:34
  496.6 36.6 %attention_backward.1 = (bf16[2048,768]{1,0:T(8,128)(2,1)}, bf16[2048,768]{1,0:T(8,128)(2,1)}, bf16[2048,768]{1,0:T(8,128)(2,1)}) custom-call(s32[4]{0:T(128)} %len_ref.3, bf16[2048,768]{1,0:T(8,128)(2,1)} %add_convert_fusion.3.q_ref, bf16[2048,768]{1,0:T(8,128)(2,1)} %convolution_convert_fusion.3.k_ref, bf16[2048,768]{1,0:T(8,128)(2,1)} %add_convert_fusion.2.v_ref, ...), custom_call_target="tpu_custom_call" | custom-call | tf_op jit(solution)/shard_map/attention_backward/pallas_call | solution.py:188
  533.2 7.4 fusion.59
  547.6 8.1 select_reduce_fusion
  558.7 18.2 %collective-permute-start.27 = (f32[22,768]{1,0:T(8,128)S(1)}, f32[22,768]{1,0:T(8,128)S(1)}, u32[]{:S(2)}, u32[]{:S(2)}) collective-permute-start(f32[22,768]{1,0:T(8,128)S(1)} %concatenate.18), channel_id=1, source_target_pairs={{0,1},{1,0},{2,3},{3,2},{4,5},{5,4},{6,7},{7,6},{8,9},{9,8},{10,11... | collective-permute-start | bytes 202760 | tf_op jit(solution)/shard_map/ppermute | solution.py:48
  600.9 5.7 gather_fusion.28
  606.6 11.6 %reshape.528 = bf16[8,96,4,2,384]{4,3,2,1,0:T(2,128)(2,1)} reshape(bf16[768,3072]{1,0:T(8,128)(2,1)} %convolution_convert_fusion.1) | data formatting | bytes 9437184 | tf_op jit(solution)/shard_map/reshape | solution.py:259
  623.7 5.8 gather_fusion.26
  629.5 8.6 broadcast_select_fusion.3
  638.1 5.8 gather_fusion.29
  660.6 6.5 collective-permute-start.37
  766.1 7.2 copy.246
  790.7 6.0 fusion.13
  806.9 15.3 %collective-permute-done.22 = bf16[4,224,384]{2,1,0:T(8,128)(2,1)} collective-permute-done((bf16[4,224,384]{2,1,0:T(8,128)(2,1)}, bf16[4,224,384]{2,1,0:T(8,128)(2,1)}, u32[]{:S(2)}, u32[]{:S(2)}) %collective-permute-start.22) | collective-permute-done | bytes 688160 | tf_op jit(solution)/shard_map/ppermute | solution.py:48
  826.7 9.0 %collective-permute-done.38 = bf16[4,384,384]{2,1,0:T(8,128)(2,1)S(1)} collective-permute-done((bf16[4,384,384]{2,1,0:T(8,128)(2,1)}, bf16[4,384,384]{2,1,0:T(8,128)(2,1)S(1)}, u32[]{:S(2)}, u32[]{:S(2)}) %collective-permute-start.38) | collective-permute-done | bytes 1179680 | tf_op jit(solution)/shard_map/ppermute | solution.py:48
  837.1 34.4 %collective-permute-done.39 = bf16[4,384,384]{2,1,0:T(8,128)(2,1)} collective-permute-done((bf16[4,384,384]{2,1,0:T(8,128)(2,1)}, bf16[4,384,384]{2,1,0:T(8,128)(2,1)}, u32[]{:S(2)}, u32[]{:S(2)}) %collective-permute-start.39) | collective-permute-done | bytes 1179680 | tf_op jit(solution)/shard_map/ppermute | solution.py:48
  887.3 11.8 %collective-permute-done.42 = bf16[384,384]{1,0:T(8,128)(2,1)S(1)} collective-permute-done((bf16[384,384]{1,0:T(8,128)(2,1)S(1)}, bf16[384,384]{1,0:T(8,128)(2,1)S(1)}, u32[]{:S(2)}, u32[]{:S(2)}) %collective-permute-start.42) | collective-permute-done | bytes 294944 | tf_op jit(solution)/shard_map/ppermute | solution.py:48
  (517 shorter events, 424.8 us)
Async XLA Ops:
  4.7 19.8 %collective-permute-start.1 = (bf16[176,384]{1,0:T(8,128)(2,1)S(1)}, bf16[176,384]{1,0:T(8,128)(2,1)S(1)}, u32[]{:S(2)}, u32[]{:S(2)}) collective-permute-start(bf16[176,384]{1,0:T(8,128)(2,1)S(1)} %constant_dynamic-update-slice_fusion), channel_id=1, source_target_pairs={{0,2},{1,3},{2,0},{3,1},{4,6},{5,7},{6,4},{7,5},{8,10},{9,11},{10,... | collective-permute-start | bytes 405512 | tf_op jit(solution)/shard_map/ppermute | solution.py:48
  8.8 16.6 %collective-permute-start.2 = (bf16[176,384]{1,0:T(8,128)(2,1)S(1)}, bf16[176,384]{1,0:T(8,128)(2,1)S(1)}, u32[]{:S(2)}, u32[]{:S(2)}) collective-permute-start(bf16[176,384]{1,0:T(8,128)(2,1)S(1)} %constant_dynamic-update-slice_fusion), channel_id=1, source_target_pairs={{0,3},{1,2},{2,1},{3,0},{4,7},{5,6},{6,5},{7,4},{8,11},{9,10},{10,... | collective-permute-start | bytes 405512 | tf_op jit(solution)/shard_map/ppermute | solution.py:48
  10.1 15.3 %collective-permute-start = (bf16[176,384]{1,0:T(8,128)(2,1)S(1)}, bf16[176,384]{1,0:T(8,128)(2,1)S(1)}, u32[]{:S(2)}, u32[]{:S(2)}) collective-permute-start(bf16[176,384]{1,0:T(8,128)(2,1)S(1)} %constant_dynamic-update-slice_fusion), channel_id=1, source_target_pairs={{0,1},{1,0},{2,3},{3,2},{4,5},{5,4},{6,7},{7,6},{8,9},{9,8},{10,11... | collective-permute-start | bytes 405512 | tf_op jit(solution)/shard_map/ppermute | solution.py:48
  13.2 18.8 %collective-permute-start.10 = (bf16[432,384]{1,0:T(8,128)(2,1)S(1)}, bf16[432,384]{1,0:T(8,128)(2,1)S(1)}, u32[]{:S(2)}, u32[]{:S(2)}) collective-permute-start(bf16[432,384]{1,0:T(8,128)(2,1)S(1)} %get-tuple-element.166), channel_id=1, source_target_pairs={{0,1},{1,0},{2,3},{3,2},{4,5},{5,4},{6,7},{7,6},{8,9},{9,8},{10,11... | collective-permute-start | bytes 995336 | tf_op jit(solution)/shard_map/ppermute | solution.py:48
  15.1 28.4 %collective-permute-start.11 = (bf16[432,384]{1,0:T(8,128)(2,1)S(1)}, bf16[432,384]{1,0:T(8,128)(2,1)}, u32[]{:S(2)}, u32[]{:S(2)}) collective-permute-start(bf16[432,384]{1,0:T(8,128)(2,1)S(1)} %get-tuple-element.166), channel_id=1, source_target_pairs={{0,2},{1,3},{2,0},{3,1},{4,6},{5,7},{6,4},{7,5},{8,10},{9,11},{10,... | collective-permute-start | bytes 995336 | tf_op jit(solution)/shard_map/ppermute | solution.py:48
  24.4 21.8 %collective-permute-start.12 = (bf16[432,384]{1,0:T(8,128)(2,1)S(1)}, bf16[432,384]{1,0:T(8,128)(2,1)S(1)}, u32[]{:S(2)}, u32[]{:S(2)}) collective-permute-start(bf16[432,384]{1,0:T(8,128)(2,1)S(1)} %get-tuple-element.166), channel_id=1, source_target_pairs={{0,3},{1,2},{2,1},{3,0},{4,7},{5,6},{6,5},{7,4},{8,11},{9,10},{10,... | collective-permute-start | bytes 995336 | tf_op jit(solution)/shard_map/ppermute | solution.py:48
  25.5 26.9 %collective-permute-start.3 = (bf16[4,176,384]{2,1,0:T(8,128)(2,1)S(1)}, bf16[4,176,384]{2,1,0:T(8,128)(2,1)S(1)}, u32[]{:S(2)}, u32[]{:S(2)}) collective-permute-start(bf16[4,176,384]{2,1,0:T(8,128)(2,1)S(1)} %pad_maximum_fusion.2), channel_id=1, source_target_pairs={{0,4},{4,0},{8,12},{12,8},{16,20},{20,16},{24,28},{28,24},{1,5},{5... | collective-permute-start | bytes 1622024 | tf_op jit(solution)/shard_map/ppermute | solution.py:48
  25.6 27.4 %collective-permute-start.4 = (bf16[4,176,384]{2,1,0:T(8,128)(2,1)S(1)}, bf16[4,176,384]{2,1,0:T(8,128)(2,1)S(1)}, u32[]{:S(2)}, u32[]{:S(2)}) collective-permute-start(bf16[4,176,384]{2,1,0:T(8,128)(2,1)S(1)} %pad_maximum_fusion.2), channel_id=1, source_target_pairs={{0,8},{4,12},{8,0},{12,4},{16,24},{20,28},{24,16},{28,20},{1,9},{5... | collective-permute-start | bytes 1622024 | tf_op jit(solution)/shard_map/ppermute | solution.py:48
  32.0 21.2 %collective-permute-start.6 = (bf16[4,176,384]{2,1,0:T(8,128)(2,1)S(1)}, bf16[4,176,384]{2,1,0:T(8,128)(2,1)S(1)}, u32[]{:S(2)}, u32[]{:S(2)}) collective-permute-start(bf16[4,176,384]{2,1,0:T(8,128)(2,1)S(1)} %pad_maximum_fusion.2), channel_id=1, source_target_pairs={{0,16},{4,20},{8,24},{12,28},{16,0},{20,4},{24,8},{28,12},{1,17},{... | collective-permute-start | bytes 1622024 | tf_op jit(solution)/shard_map/ppermute | solution.py:48
  43.4 14.8 %collective-permute-start.8 = (bf16[4,176,384]{2,1,0:T(8,128)(2,1)S(1)}, bf16[4,176,384]{2,1,0:T(8,128)(2,1)S(1)}, u32[]{:S(2)}, u32[]{:S(2)}) collective-permute-start(bf16[4,176,384]{2,1,0:T(8,128)(2,1)S(1)} %pad_maximum_fusion.2), channel_id=1, source_target_pairs={{0,24},{4,28},{8,16},{12,20},{16,8},{20,12},{24,0},{28,4},{1,25},{... | collective-permute-start | bytes 1622024 | tf_op jit(solution)/shard_map/ppermute | solution.py:48
  48.4 66.8 %collective-permute-start.13 = (bf16[4,432,384]{2,1,0:T(8,128)(2,1)}, bf16[4,432,384]{2,1,0:T(8,128)(2,1)}, u32[]{:S(2)}, u32[]{:S(2)}) collective-permute-start(bf16[4,432,384]{2,1,0:T(8,128)(2,1)} %pad_maximum_fusion.1), channel_id=1, source_target_pairs={{0,4},{4,0},{8,12},{12,8},{16,20},{20,16},{24,28},{28,24},{1,5},{5... | collective-permute-start | bytes 3981320 | tf_op jit(solution)/shard_map/ppermute | solution.py:48
  52.4 34.0 %collective-permute-start.14 = (bf16[4,432,384]{2,1,0:T(8,128)(2,1)}, bf16[4,432,384]{2,1,0:T(8,128)(2,1)}, u32[]{:S(2)}, u32[]{:S(2)}) collective-permute-start(bf16[4,432,384]{2,1,0:T(8,128)(2,1)} %pad_maximum_fusion.1), channel_id=1, source_target_pairs={{0,8},{4,12},{8,0},{12,4},{16,24},{20,28},{24,16},{28,20},{1,9},{5... | collective-permute-start | bytes 3981320 | tf_op jit(solution)/shard_map/ppermute | solution.py:48
  58.2 56.5 %collective-permute-start.16 = (bf16[4,432,384]{2,1,0:T(8,128)(2,1)}, bf16[4,432,384]{2,1,0:T(8,128)(2,1)}, u32[]{:S(2)}, u32[]{:S(2)}) collective-permute-start(bf16[4,432,384]{2,1,0:T(8,128)(2,1)} %pad_maximum_fusion.1), channel_id=1, source_target_pairs={{0,16},{4,20},{8,24},{12,28},{16,0},{20,4},{24,8},{28,12},{1,17},{... | collective-permute-start | bytes 3981320 | tf_op jit(solution)/shard_map/ppermute | solution.py:48
  59.4 55.4 %collective-permute-start.18 = (bf16[4,432,384]{2,1,0:T(8,128)(2,1)}, bf16[4,432,384]{2,1,0:T(8,128)(2,1)}, u32[]{:S(2)}, u32[]{:S(2)}) collective-permute-start(bf16[4,432,384]{2,1,0:T(8,128)(2,1)} %pad_maximum_fusion.1), channel_id=1, source_target_pairs={{0,24},{4,28},{8,16},{12,20},{16,8},{20,12},{24,0},{28,4},{1,25},{... | collective-permute-start | bytes 3981320 | tf_op jit(solution)/shard_map/ppermute | solution.py:48
  86.4 36.9 %collective-permute-start.15 = (bf16[4,432,384]{2,1,0:T(8,128)(2,1)}, bf16[4,432,384]{2,1,0:T(8,128)(2,1)}, u32[]{:S(2)}, u32[]{:S(2)}) collective-permute-start(bf16[4,432,384]{2,1,0:T(8,128)(2,1)} %collective-permute-done.14), channel_id=1, source_target_pairs={{0,4},{4,0},{8,12},{12,8},{16,20},{20,16},{24,28},{28,24},{1,5},{5... | collective-permute-start | bytes 3981320 | tf_op jit(solution)/shard_map/ppermute | solution.py:48
  558.7 173.2 %collective-permute-start.27 = (f32[22,768]{1,0:T(8,128)S(1)}, f32[22,768]{1,0:T(8,128)S(1)}, u32[]{:S(2)}, u32[]{:S(2)}) collective-permute-start(f32[22,768]{1,0:T(8,128)S(1)} %concatenate.18), channel_id=1, source_target_pairs={{0,1},{1,0},{2,3},{3,2},{4,5},{5,4},{6,7},{7,6},{8,9},{9,8},{10,11... | collective-permute-start | bytes 202760 | tf_op jit(solution)/shard_map/ppermute | solution.py:48
  576.9 156.6 %collective-permute-start.28 = (f32[22,768]{1,0:T(8,128)S(1)}, f32[22,768]{1,0:T(8,128)S(1)}, u32[]{:S(2)}, u32[]{:S(2)}) collective-permute-start(f32[22,768]{1,0:T(8,128)S(1)} %concatenate.18), channel_id=1, source_target_pairs={{0,2},{1,3},{2,0},{3,1},{4,6},{5,7},{6,4},{7,5},{8,10},{9,11},{10,... | collective-permute-start | bytes 202760 | tf_op jit(solution)/shard_map/ppermute | solution.py:48
  578.6 154.9 %collective-permute-start.29 = (f32[22,768]{1,0:T(8,128)S(1)}, f32[22,768]{1,0:T(8,128)S(1)}, u32[]{:S(2)}, u32[]{:S(2)}) collective-permute-start(f32[22,768]{1,0:T(8,128)S(1)} %concatenate.18), channel_id=1, source_target_pairs={{0,3},{1,2},{2,1},{3,0},{4,7},{5,6},{6,5},{7,4},{8,11},{9,10},{10,... | collective-permute-start | bytes 202760 | tf_op jit(solution)/shard_map/ppermute | solution.py:48
  660.6 130.1 %collective-permute-start.37 = (bf16[4,4,384,384]{3,2,1,0:T(8,128)(2,1)}, bf16[4,4,384,384]{3,2,1,0:T(8,128)(2,1)}, u32[]{:S(2)}, u32[]{:S(2)}) collective-permute-start(bf16[4,4,384,384]{3,2,1,0:T(8,128)(2,1)} %copy_bitcast_fusion), channel_id=1, source_target_pairs={{0,4},{4,0},{8,12},{12,8},{16,20},{20,16},{24,28},{28,24},{1,5},{5... | collective-permute-start | bytes 14155784 | tf_op jit(solution)/shard_map/ppermute | solution.py:48
  731.8 41.5 %collective-permute-start.20 = (bf16[4,4,224,384]{3,2,1,0:T(8,128)(2,1)}, bf16[4,4,224,384]{3,2,1,0:T(8,128)(2,1)}, u32[]{:S(2)}, u32[]{:S(2)}) collective-permute-start(bf16[4,4,224,384]{3,2,1,0:T(8,128)(2,1)} %copy_bitcast_fusion.3), channel_id=1, source_target_pairs={{0,4},{4,0},{8,12},{12,8},{16,20},{20,16},{24,28},{28,24},{1,5},{5... | collective-permute-start | bytes 8257544 | tf_op jit(solution)/shard_map/ppermute | solution.py:48
  734.5 14.3 %collective-permute-start.33 = (f32[4,22,768]{2,0,1:T(4,128)S(1)}, f32[4,22,768]{2,0,1:T(4,128)S(1)}, u32[]{:S(2)}, u32[]{:S(2)}) collective-permute-start(f32[4,22,768]{2,0,1:T(4,128)S(1)} %pad_maximum_fusion.4), channel_id=1, source_target_pairs={{0,16},{4,20},{8,24},{12,28},{16,0},{20,4},{24,8},{28,12},{1,17},{... | collective-permute-start | bytes 811016 | tf_op jit(solution)/shard_map/ppermute | solution.py:48
  777.1 21.5 %collective-permute-start.21 = (bf16[4,224,384]{2,1,0:T(8,128)(2,1)}, bf16[4,224,384]{2,1,0:T(8,128)(2,1)}, u32[]{:S(2)}, u32[]{:S(2)}) collective-permute-start(bf16[4,224,384]{2,1,0:T(8,128)(2,1)} %get-tuple-element.106), channel_id=1, source_target_pairs={{0,8},{4,12},{8,0},{12,4},{16,24},{20,28},{24,16},{28,20},{1,9},{5... | collective-permute-start | bytes 2064392 | tf_op jit(solution)/shard_map/ppermute | solution.py:48
  788.8 33.4 %collective-permute-start.22 = (bf16[4,224,384]{2,1,0:T(8,128)(2,1)}, bf16[4,224,384]{2,1,0:T(8,128)(2,1)}, u32[]{:S(2)}, u32[]{:S(2)}) collective-permute-start(bf16[4,224,384]{2,1,0:T(8,128)(2,1)} %get-tuple-element.108), channel_id=1, source_target_pairs={{0,16},{4,20},{8,24},{12,28},{16,0},{20,4},{24,8},{28,12},{1,17},{... | collective-permute-start | bytes 2064392 | tf_op jit(solution)/shard_map/ppermute | solution.py:48
  789.1 33.1 %collective-permute-start.23 = (bf16[4,224,384]{2,1,0:T(8,128)(2,1)S(1)}, bf16[4,224,384]{2,1,0:T(8,128)(2,1)}, u32[]{:S(2)}, u32[]{:S(2)}) collective-permute-start(bf16[4,224,384]{2,1,0:T(8,128)(2,1)S(1)} %get-tuple-element.107), channel_id=1, source_target_pairs={{0,24},{4,28},{8,16},{12,20},{16,8},{20,12},{24,0},{28,4},{1,25},{... | collective-permute-start | bytes 2064392 | tf_op jit(solution)/shard_map/ppermute | solution.py:48
  796.7 39.0 %collective-permute-start.38 = (bf16[4,384,384]{2,1,0:T(8,128)(2,1)}, bf16[4,384,384]{2,1,0:T(8,128)(2,1)S(1)}, u32[]{:S(2)}, u32[]{:S(2)}) collective-permute-start(bf16[4,384,384]{2,1,0:T(8,128)(2,1)} %get-tuple-element.103), channel_id=1, source_target_pairs={{0,8},{4,12},{8,0},{12,4},{16,24},{20,28},{24,16},{28,20},{1,9},{5... | collective-permute-start | bytes 3538952 | tf_op jit(solution)/shard_map/ppermute | solution.py:48
  798.1 73.4 %collective-permute-start.39 = (bf16[4,384,384]{2,1,0:T(8,128)(2,1)}, bf16[4,384,384]{2,1,0:T(8,128)(2,1)}, u32[]{:S(2)}, u32[]{:S(2)}) collective-permute-start(bf16[4,384,384]{2,1,0:T(8,128)(2,1)} %get-tuple-element.105), channel_id=1, source_target_pairs={{0,16},{4,20},{8,24},{12,28},{16,0},{20,4},{24,8},{28,12},{1,17},{... | collective-permute-start | bytes 3538952 | tf_op jit(solution)/shard_map/ppermute | solution.py:48
  798.6 72.9 %collective-permute-start.40 = (bf16[4,384,384]{2,1,0:T(8,128)(2,1)}, bf16[4,384,384]{2,1,0:T(8,128)(2,1)}, u32[]{:S(2)}, u32[]{:S(2)}) collective-permute-start(bf16[4,384,384]{2,1,0:T(8,128)(2,1)} %get-tuple-element.104), channel_id=1, source_target_pairs={{0,24},{4,28},{8,16},{12,20},{16,8},{20,12},{24,0},{28,4},{1,25},{... | collective-permute-start | bytes 3538952 | tf_op jit(solution)/shard_map/ppermute | solution.py:48
  824.6 52.2 %collective-permute-start.24 = (bf16[224,384]{1,0:T(8,128)(2,1)S(1)}, bf16[224,384]{1,0:T(8,128)(2,1)S(1)}, u32[]{:S(2)}, u32[]{:S(2)}) collective-permute-start(bf16[224,384]{1,0:T(8,128)(2,1)S(1)} %get-tuple-element.132), channel_id=1, source_target_pairs={{0,1},{1,0},{2,3},{3,2},{4,5},{5,4},{6,7},{7,6},{8,9},{9,8},{10,11... | collective-permute-start | bytes 516104 | tf_op jit(solution)/shard_map/ppermute | solution.py:48
  825.5 53.8 %collective-permute-start.25 = (bf16[224,384]{1,0:T(8,128)(2,1)S(1)}, bf16[224,384]{1,0:T(8,128)(2,1)S(1)}, u32[]{:S(2)}, u32[]{:S(2)}) collective-permute-start(bf16[224,384]{1,0:T(8,128)(2,1)S(1)} %get-tuple-element.134), channel_id=1, source_target_pairs={{0,2},{1,3},{2,0},{3,1},{4,6},{5,7},{6,4},{7,5},{8,10},{9,11},{10,... | collective-permute-start | bytes 516104 | tf_op jit(solution)/shard_map/ppermute | solution.py:48
  835.7 43.6 %collective-permute-start.26 = (bf16[224,384]{1,0:T(8,128)(2,1)S(1)}, bf16[224,384]{1,0:T(8,128)(2,1)S(1)}, u32[]{:S(2)}, u32[]{:S(2)}) collective-permute-start(bf16[224,384]{1,0:T(8,128)(2,1)S(1)} %get-tuple-element.133), channel_id=1, source_target_pairs={{0,3},{1,2},{2,1},{3,0},{4,7},{5,6},{6,5},{7,4},{8,11},{9,10},{10,... | collective-permute-start | bytes 516104 | tf_op jit(solution)/shard_map/ppermute | solution.py:48
  875.7 23.4 %collective-permute-start.42 = (bf16[384,384]{1,0:T(8,128)(2,1)S(1)}, bf16[384,384]{1,0:T(8,128)(2,1)S(1)}, u32[]{:S(2)}, u32[]{:S(2)}) collective-permute-start(bf16[384,384]{1,0:T(8,128)(2,1)S(1)} %get-tuple-element.131), channel_id=1, source_target_pairs={{0,2},{1,3},{2,0},{3,1},{4,6},{5,7},{6,4},{7,5},{8,10},{9,11},{10,... | collective-permute-start | bytes 884744 | tf_op jit(solution)/shard_map/ppermute | solution.py:48
  876.9 22.2 %collective-permute-start.43 = (bf16[384,384]{1,0:T(8,128)(2,1)S(1)}, bf16[384,384]{1,0:T(8,128)(2,1)S(1)}, u32[]{:S(2)}, u32[]{:S(2)}) collective-permute-start(bf16[384,384]{1,0:T(8,128)(2,1)S(1)} %get-tuple-element.130), channel_id=1, source_target_pairs={{0,3},{1,2},{2,1},{3,0},{4,7},{5,6},{6,5},{7,4},{8,11},{9,10},{10,... | collective-permute-start | bytes 884744 | tf_op jit(solution)/shard_map/ppermute | solution.py:48
  (104 other events, 1914.9 us)
